TPU v7x, 512 devices: a whole 4x4x16 slice. The times are simulated.
512 devices in a mesh: shot: 16 (over z_hi, y), slab: 32 (over z_lo, x, core).
Axes of the slice: x: 4, y: 4, z: 16 (z_hi: 4, z_lo: 4; z = z_hi * 4 + z_lo), core: 2. Of those that a mesh axis runs over, the one named last changes fastest.
Arguments:
- wave_now: float32 [16, 512, 64, 128], P('shot', 'slab'), may hold values from -6 to 6
- wave_prev: float32 [16, 512, 64, 128], P('shot', 'slab'), may hold values from -6 to 6
- courant: float32 [512, 64, 128], P('slab'), may hold values from 0.05 to 0.2
- forward: bfloat16 [16, 3, 512, 64, 128], P('shot', None, 'slab'), may hold values from -6 to 6
- receivers: int32 [16, 3, 256], P('shot'), may hold values from 0 to 511, as said below
- residual: float32 [16, 3, 256], P('shot'), may hold values from -6 to 6
- aperture: int32 [16, 2], P('shot'), may hold values from 0 to 512, as said below
- latent: bfloat16 [256, 32, 4096], P('slab', 'shot')
- weight: float32 [64, 8], replicated, may hold values from -0.75 to 0.75
Outputs:
- wave_after: float32 [16, 512, 64, 128], P('shot', 'slab')
- wave_before: float32 [16, 512, 64, 128], P('shot', 'slab')
- latent_grad: float32 [256, 32, 4096], P('slab', 'shot')
- weight_grad: float32 [64, 8], replicated
Inputs may be any that keep to these rules, and one draw needn't show every extreme that they name: receivers[s,0,r], receivers[s,1,r], receivers[s,2,r] are an x, y and depth cell inside the grid. Each shot's aperture is a range of at least 512 // 4 x cells with aperture[s,0] < aperture[s,1].
All inputs are finite; a program needn't handle non-finite values.
Results may differ from a plain program's by a relative error of at most 0.0003.
Values sent between devices are 32-bit elements; how exact they have to be, the bound alone decides.
No kernel may reach another device: no remote copies, remote signals or barrier semaphores. Data moves between devices by JAX's collectives and lax.ppermute only.
A program may use at most 64 MiB of HBM per device.

v0:
```python
import math
import jax
import jax.numpy as jnp
from jax import lax
from jax.sharding import PartitionSpec as P

STEPS = 3
stencil_weights = (-205.0 / 72.0, 8.0 / 5.0, -1.0 / 5.0, 8.0 / 315.0, -1.0 / 560.0)


def extended(block, sides, width):
    for axis, dim in sides:
        count = lax.axis_size(axis)
        forward = [(i, i + 1) for i in range(count - 1)]
        backward = [(target, source) for source, target in forward]
        low = lax.ppermute(
            lax.slice_in_dim(block, block.shape[dim] - width, None, axis=dim), axis, forward
        )
        high = lax.ppermute(lax.slice_in_dim(block, 0, width, axis=dim), axis, backward)
        block = jnp.concatenate([low, block, high], axis=dim)
    return block


def laplace(padded):
    size_x = padded.shape[0] - 8
    size_y = padded.shape[1] - 8
    size_z = padded.shape[2] - 8

    def moved(shift_x, shift_y, shift_z):
        return padded[
            4 + shift_x : 4 + shift_x + size_x,
            4 + shift_y : 4 + shift_y + size_y,
            4 + shift_z : 4 + shift_z + size_z,
        ]

    total = 3.0 * stencil_weights[0] * moved(0, 0, 0)
    for offset in range(1, 5):
        cycle_sum = moved(offset, 0, 0) + moved(-offset, 0, 0)
        cycle_sum = cycle_sum + moved(0, offset, 0) + moved(0, -offset, 0)
        cycle_sum = cycle_sum + moved(0, 0, offset) + moved(0, 0, -offset)
        total = total + stencil_weights[offset] * cycle_sum
    return total


def pad_sides(field):
    return jnp.pad(field, ((0, 0), (4, 4), (4, 4)))


def inject(field, receivers, values, first_x):
    extent = field.shape[0]
    local_x = receivers[0, 0] - first_x
    valid = (local_x >= 0) & (local_x < extent)
    local_x = jnp.where(valid, local_x, extent)
    return field.at[local_x, receivers[0, 1], receivers[0, 2]].add(values, mode="drop")


def body(wave_now, wave_prev, courant, forward, receivers, residual, aperture, latent, weight):
    slab_cells = courant.shape[0]
    first_x = lax.axis_index("slab") * slab_cells
    current = wave_now[0]
    previous = wave_prev[0]
    accum = jnp.zeros(current.shape, jnp.float32)
    for instant in range(STEPS):
        padded = extended(current, (("slab", 0),), 4)
        advanced = 2.0 * current - previous + courant * laplace(pad_sides(padded))
        advanced = inject(advanced, receivers, residual[0, instant], first_x)
        accum = accum + advanced * forward[0, instant].astype(jnp.float32)
        previous = current
        current = advanced
    x_cells = first_x + jnp.arange(slab_cells, dtype=jnp.int32)
    inside = (x_cells >= aperture[0, 0]) & (x_cells < aperture[0, 1])
    image = jnp.where(inside[:, None, None], courant * accum, 0.0)
    image_rows = image.transpose(1, 0, 2)
    tile_rows = image_rows.shape[0] // lax.axis_size("shot")
    tile = lax.psum_scatter(image_rows, "shot", scatter_dimension=0, tiled=True).transpose(1, 0, 2)
    half_x = slab_cells // 2
    half_y = tile_rows // 2
    half_z = tile.shape[2] // 2
    taps = (
        tile.reshape(half_x, 2, half_y, 2, half_z, 2)
        .transpose(0, 2, 4, 1, 3, 5)
        .reshape(half_x, half_y, half_z, 8)
    )
    channels = weight.shape[0]
    latent_grad = jnp.einsum(
        "ijkq,cq->ijck", taps, weight, precision=lax.Precision.HIGHEST
    ).reshape(half_x, half_y, channels * half_z)
    latent_wide = latent.astype(jnp.float32).reshape(half_x, half_y, channels, half_z)
    partial_grad = jnp.einsum("ijck,ijkq->cq", latent_wide, taps, precision=lax.Precision.HIGHEST)
    latent_cells = (
        latent.shape[0] * lax.axis_size("slab") * latent.shape[1] * lax.axis_size("shot") * half_z
    )
    weight_grad = lax.psum(partial_grad, ("shot", "slab")) * (1.0 / math.sqrt(latent_cells))
    return (current[None], previous[None], latent_grad, weight_grad)


def solution(mesh):
    return jax.shard_map(
        body,
        mesh=mesh,
        in_specs=(
            P("shot", "slab", None, None),
            P("shot", "slab", None, None),
            P("slab", None, None),
            P("shot", None, "slab", None, None),
            P("shot", None, None),
            P("shot", None, None),
            P("shot", None),
            P("slab", "shot", None),
            P(),
        ),
        out_specs=(
            P("shot", "slab", None, None),
            P("shot", "slab", None, None),
            P("slab", "shot", None),
            P(),
        ),
        check_vma=False,
    )
```

profile of v0, /device:TPU:1, one launch (start us, length us, event | category | flops | bytes accessed | tf_op | source)
XLA Modules:
  0.0 334.7 jit_solution(5647150959445888792)
XLA Ops:
  7.2 0.0 copy-start
  7.2 0.0 copy-start.4
  7.2 0.0 copy-start.3
  7.2 0.0 reduce-scatter.2.cloned.1.call-start
  7.2 1.1 slice_bitcast_fusion.1
  8.3 8.8 %collective-permute-start = (f32[4,64,128]{2,1,0:T(8,128)S(1)}, f32[4,64,128]{2,1,0:T(8,128)S(1)}, u32[]{:S(2)}, u32[]{:S(2)}) collective-permute-start(f32[4,64,128]{2,1,0:T(8,128)S(1)} %get-tuple-element.24), channel_id=1, source_target_pairs={{1,0},{2,1},{3,2},{4,3},{5,4},{6,5},{7,6},{8,7},{9,8},{10,9},{11,1... | collective-permute-start | bytes 393224 | tf_op jit(solution)/shard_map/ppermute | solution.py:19
  17.1 1.9 collective-permute-start.1
  19.0 0.7 fusion.67
  19.8 0.7 or_select_fusion
  20.5 0.0 collective-permute-done
  20.5 0.5 collective-permute-done.1
  21.0 0.0 copy-start.6
  21.0 0.7 copy-done.6
  21.6 1.6 select_maximum_fusion.4
  23.2 0.0 copy-done.4
  23.2 0.0 copy-done.3
  23.2 3.7 %fusion.13 = f32[16,64,128]{2,1,0:T(8,128)S(1)} fusion(f32[16,64,128]{2,1,0:T(8,128)S(1)} %copy-done.3, f32[16,64,128]{2,1,0:T(8,128)S(1)} %bitcast.63, f32[4,64,128]{2,1,0:T(8,128)} %copy-done.6, f32[4,64,128]{2,1,0:T(8,128)S(1)} %collective-permute-done, f32[24,72,136]{2,1,0:T(8,128)S(1)} %select_maximum_fusion.4, f32[1,16,64,128]{3,2,1,0:T(8,128)} %param.10), kind=kLoop, calls=%fused_computation.40 | loop fusion | flops 5373952 | bytes 10747904 | tf_op jit(solution)/shard_map/add | solution.py:65
  26.9 15.6 %scatter_fusion = f32[16,64,128]{2,1,0:T(8,128)S(1)} fusion(f32[16,64,128]{2,1,0:T(8,128)S(1)} %fusion.13, s32[256]{0:T(256)S(1)} %bitcast.56, f32[256]{0:T(256)S(1)} %bitcast.69), kind=kCustom, calls=%fused_computation | custom fusion | flops 256 | bytes 6144 | tf_op jit(solution)/shard_map/scatter-add | solution.py:54
  42.5 4.3 %collective-permute-start.3 = (f32[4,64,128]{2,1,0:T(8,128)S(1)}, f32[4,64,128]{2,1,0:T(8,128)S(1)}, u32[]{:S(2)}, u32[]{:S(2)}) collective-permute-start(f32[4,64,128]{2,1,0:T(8,128)S(1)} %get-tuple-element.22), channel_id=1, source_target_pairs={{0,1},{1,2},{2,3},{3,4},{4,5},{5,6},{6,7},{7,8},{8,9},{9,10},{10,1... | collective-permute-start | bytes 393224 | tf_op jit(solution)/shard_map/ppermute | solution.py:16
  46.8 1.9 collective-permute-start.2
  48.8 0.0 collective-permute-done.3
  48.8 0.1 constant_dynamic-update-slice_fusion.1
  48.9 4.2 %collective-permute-done.2 = f32[4,64,128]{2,1,0:T(8,128)S(1)} collective-permute-done((f32[4,64,128]{2,1,0:T(8,128)S(1)}, f32[4,64,128]{2,1,0:T(8,128)S(1)}, u32[]{:S(2)}, u32[]{:S(2)}) %collective-permute-start.2) | collective-permute-done | bytes 131104 | tf_op jit(solution)/shard_map/ppermute | solution.py:19
  53.1 0.5 select_maximum_fusion.2
  53.7 2.1 fusion.46
  55.8 0.0 copy-start.8
  55.8 15.6 %scatter_fusion.1 = f32[16,64,128]{2,1,0:T(8,128)S(1)} fusion(f32[16,64,128]{2,1,0:T(8,128)S(1)} %fusion.46, s32[256]{0:T(256)S(1)} %bitcast.57, f32[256]{0:T(256)S(1)} %bitcast.68), kind=kCustom, calls=%fused_computation.1 | custom fusion | flops 256 | bytes 6144 | tf_op jit(solution)/shard_map/scatter-add | solution.py:54
  71.4 0.0 copy-start.1
  71.4 1.9 collective-permute-start.5
  73.3 0.0 copy-done.8
  73.3 0.6 fusion.68
  73.9 1.3 compare_and_fusion
  75.2 2.6 collective-permute-start.4
  77.8 0.0 collective-permute-done.5
  77.8 0.1 constant_dynamic-update-slice_fusion.5
  78.0 3.5 %collective-permute-done.4 = f32[4,64,128]{2,1,0:T(8,128)S(1)} collective-permute-done((f32[4,64,128]{2,1,0:T(8,128)S(1)}, f32[4,64,128]{2,1,0:T(8,128)S(1)}, u32[]{:S(2)}, u32[]{:S(2)}) %collective-permute-start.4) | collective-permute-done | bytes 131104 | tf_op jit(solution)/shard_map/ppermute | solution.py:19
  81.5 0.5 select_maximum_fusion
  82.1 2.1 fusion.36
  84.2 0.0 copy-start.5
  84.2 15.6 %scatter_fusion.2 = f32[16,64,128]{2,1,0:T(8,128)S(1)} fusion(f32[16,64,128]{2,1,0:T(8,128)S(1)} %fusion.36, s32[256]{0:T(256)S(1)} %bitcast.58, f32[256]{0:T(256)S(1)} %bitcast.67), kind=kCustom, calls=%fused_computation.2 | custom fusion | flops 256 | bytes 6144 | tf_op jit(solution)/shard_map/scatter-add | solution.py:54
  99.7 0.0 copy-done.1
  99.7 0.0 copy-done.5
  99.8 0.0 copy-start.2
  99.8 0.0 copy-start.7
  99.8 0.3 fusion.58
  100.1 1.1 copy.23
  101.2 0.0 copy-done.2
  101.2 0.0 reduce-scatter.2.cloned.1.call-update
  101.2 0.0 copy-done.7
  101.2 0.2 reshape.127
  101.4 118.1 %reduce-scatter.2.cloned.1.call-done = f32[4,16,128]{2,1,0:T(8,128)} async-done(((f32[64,16,128]{2,1,0:T(8,128)}), f32[4,16,128]{2,1,0:T(8,128)}) %reduce-scatter.2.cloned.1.call-update) | async-done | bytes 32784 | tf_op jit(solution)/shard_map/reduce_scatter | solution.py:75
  219.6 2.8 reshape.124
  222.4 0.7 copy.24
  223.1 0.0 copy-done
  223.1 1.0 convolution_bitcast_fusion
  224.1 0.2 copy.31
  224.3 1.0 reshape.151
  225.3 0.3 convolution_bitcast_fusion.1
  225.6 101.6 %psum.7 = f32[64,8]{0,1:T(8,128)S(1)} all-reduce(f32[64,8]{0,1:T(8,128)S(1)} %convolution_bitcast_fusion.1), channel_id=1, replica_groups=mesh['shot'=16,'slab'=32] {'shot','slab'}, use_global_device_ids=true, to_apply=%region_4.5 | all-reduce | flops 512 | bytes 4096 | tf_op jit(solution)/shard_map/psum | solution.py:93
  327.2 0.6 broadcast_multiply_fusion
  (6 shorter events, 0.1 us)
Async XLA Ops:
  7.2 215.9 %copy-start = (f32[64,8]{0,1:T(8,128)S(1)}, f32[64,8]{0,1:T(8,128)}, u32[]{:S(2)}) copy-start(f32[64,8]{0,1:T(8,128)} %param.17) | copy-start | bytes 6148
  7.2 16.0 %copy-start.4 = (f32[1,16,64,128]{3,2,1,0:T(8,128)S(1)}, f32[1,16,64,128]{3,2,1,0:T(8,128)}, u32[]{:S(2)}) copy-start(f32[1,16,64,128]{3,2,1,0:T(8,128)} %param.9) | copy-start | bytes 1572868
  7.2 16.0 %copy-start.3 = (f32[16,64,128]{2,1,0:T(8,128)S(1)}, f32[16,64,128]{2,1,0:T(8,128)}, u32[]{:S(2)}) copy-start(f32[16,64,128]{2,1,0:T(8,128)} %param.11) | copy-start | bytes 1572868
  7.2 212.3 %reduce-scatter.2.cloned.1.call-start = ((), (), s32[]{:S(2)}) async-start(), calls=%async_computation.1 | async-start | bytes 557056 | tf_op jit(solution)/shard_map/reduce_scatter | solution.py:75
  8.3 12.2 %collective-permute-start = (f32[4,64,128]{2,1,0:T(8,128)S(1)}, f32[4,64,128]{2,1,0:T(8,128)S(1)}, u32[]{:S(2)}, u32[]{:S(2)}) collective-permute-start(f32[4,64,128]{2,1,0:T(8,128)S(1)} %get-tuple-element.24), channel_id=1, source_target_pairs={{1,0},{2,1},{3,2},{4,3},{5,4},{6,5},{7,6},{8,7},{9,8},{10,9},{11,1... | collective-permute-start | bytes 393224 | tf_op jit(solution)/shard_map/ppermute | solution.py:19
  17.1 3.9 %collective-permute-start.1 = (f32[4,64,128]{2,1,0:T(8,128)S(1)}, f32[4,64,128]{2,1,0:T(8,128)S(1)}, u32[]{:S(2)}, u32[]{:S(2)}) collective-permute-start(f32[4,64,128]{2,1,0:T(8,128)S(1)} %get-tuple-element.25), channel_id=1, source_target_pairs={{0,1},{1,2},{2,3},{3,4},{4,5},{5,6},{6,7},{7,8},{8,9},{9,10},{10,1... | collective-permute-start | bytes 393224 | tf_op jit(solution)/shard_map/ppermute | solution.py:16
  21.0 0.7 copy-start.6
  42.5 6.3 %collective-permute-start.3 = (f32[4,64,128]{2,1,0:T(8,128)S(1)}, f32[4,64,128]{2,1,0:T(8,128)S(1)}, u32[]{:S(2)}, u32[]{:S(2)}) collective-permute-start(f32[4,64,128]{2,1,0:T(8,128)S(1)} %get-tuple-element.22), channel_id=1, source_target_pairs={{0,1},{1,2},{2,3},{3,4},{4,5},{5,6},{6,7},{7,8},{8,9},{9,10},{10,1... | collective-permute-start | bytes 393224 | tf_op jit(solution)/shard_map/ppermute | solution.py:16
  46.8 6.3 %collective-permute-start.2 = (f32[4,64,128]{2,1,0:T(8,128)S(1)}, f32[4,64,128]{2,1,0:T(8,128)S(1)}, u32[]{:S(2)}, u32[]{:S(2)}) collective-permute-start(f32[4,64,128]{2,1,0:T(8,128)S(1)} %get-tuple-element.23), channel_id=1, source_target_pairs={{1,0},{2,1},{3,2},{4,3},{5,4},{6,5},{7,6},{8,7},{9,8},{10,9},{11,1... | collective-permute-start | bytes 393224 | tf_op jit(solution)/shard_map/ppermute | solution.py:19
  55.8 17.5 %copy-start.8 = (s32[1,2]{1,0:T(1,128)S(1)}, s32[1,2]{1,0:T(1,128)}, u32[]{:S(2)}) copy-start(s32[1,2]{1,0:T(1,128)} %param.15) | copy-start | bytes 28
  71.4 28.4 %copy-start.1 = (f32[16,64,128]{2,1,0:T(8,128)}, f32[16,64,128]{2,1,0:T(8,128)S(1)}, u32[]{:S(2)}) copy-start(f32[16,64,128]{2,1,0:T(8,128)S(1)} %scatter_fusion.1) | copy-start | bytes 1572868
  71.4 6.4 %collective-permute-start.5 = (f32[4,64,128]{2,1,0:T(8,128)S(1)}, f32[4,64,128]{2,1,0:T(8,128)S(1)}, u32[]{:S(2)}, u32[]{:S(2)}) collective-permute-start(f32[4,64,128]{2,1,0:T(8,128)S(1)} %get-tuple-element.18), channel_id=1, source_target_pairs={{0,1},{1,2},{2,3},{3,4},{4,5},{5,6},{6,7},{7,8},{8,9},{9,10},{10,1... | collective-permute-start | bytes 393224 | tf_op jit(solution)/shard_map/ppermute | solution.py:16
  75.2 6.3 %collective-permute-start.4 = (f32[4,64,128]{2,1,0:T(8,128)S(1)}, f32[4,64,128]{2,1,0:T(8,128)S(1)}, u32[]{:S(2)}, u32[]{:S(2)}) collective-permute-start(f32[4,64,128]{2,1,0:T(8,128)S(1)} %get-tuple-element.19), channel_id=1, source_target_pairs={{1,0},{2,1},{3,2},{4,3},{5,4},{6,5},{7,6},{8,7},{9,8},{10,9},{11,1... | collective-permute-start | bytes 393224 | tf_op jit(solution)/shard_map/ppermute | solution.py:19
  84.2 15.6 %copy-start.5 = (bf16[1,3,16,64,128]{4,3,2,1,0:T(8,128)(2,1)S(1)}, bf16[1,3,16,64,128]{4,3,2,1,0:T(8,128)(2,1)}, u32[]{:S(2)}) copy-start(bf16[1,3,16,64,128]{4,3,2,1,0:T(8,128)(2,1)} %param.12) | copy-start | bytes 2359300
  99.8 1.4 copy-start.2
  99.8 1.4 copy-start.7
Sparse Core Ops, SparseCore 0:
  101.3 118.1 reduce-scatter.1
where the time goes:
time: 335 us
  waiting for transfers between devices  126 us (38%)
  blocking collectives  102 us (30%)
  other arithmetic  60 us (18%)
  starting transfers between devices  21.5 us (6%)
  between operations  14.4 us (4%)
  local copies, waits for them, and re-layouts  9.37 us (3%)
    reduce_scatter x1, waiting for transfers between devices, body(): lax.psum_scatter(image_rows, 'shot', scatter_dimension=0, tiled=True)  118 us
    psum x1, blocking collectives, body(): lax.psum(partial_grad, ('shot', 'slab')) * (1.0 / math.sqrt(latent_cells))  102 us
    scatter-add x3, other arithmetic, inject(): field.at[local_x, receivers[0, 1], receivers[0, 2]].add(values, mode='drop')  46.7 us
    ppermute x3, starting transfers between devices, extended(): lax.ppermute(lax.slice_in_dim(block, 0, width, axis=dim), axis, backward)  13.3 us
    ppermute x3, starting transfers between devices, extended(): lax.ppermute(lax.slice_in_dim(block, block.shape[dim] - width, None, axis...  8.19 us
    add x3, other arithmetic, body(): advanced = 2.0 * current - previous + courant * laplace(pad_sides(padded))  7.87 us
    ppermute x3, waiting for transfers between devices, extended(): lax.ppermute(lax.slice_in_dim(block, 0, width, axis=dim), axis, backward)  7.76 us
  transfers between devices with their start and end apart: 7, of which 4 were waited for; matrix products, arithmetic and copies ran while one was open for 1% of the time, Pallas kernels for 0%

commit v1 on v0

--- a/solution.py
+++ b/solution.py
@@ -3,6 +3,7 @@
 import jax.numpy as jnp
 from jax import lax
 from jax.sharding import PartitionSpec as P
+from jax.lax import all_gather
 
 STEPS = 3
 stencil_weights = (-205.0 / 72.0, 8.0 / 5.0, -1.0 / 5.0, 8.0 / 315.0, -1.0 / 560.0)
@@ -90,7 +91,9 @@
     latent_cells = (
         latent.shape[0] * lax.axis_size("slab") * latent.shape[1] * lax.axis_size("shot") * half_z
     )
-    weight_grad = lax.psum(partial_grad, ("shot", "slab")) * (1.0 / math.sqrt(latent_cells))
+    weight_grad = jnp.sum(all_gather(partial_grad, ("shot", "slab")), axis=0) * (
+        1.0 / math.sqrt(latent_cells)
+    )
     return (current[None], previous[None], latent_grad, weight_grad)
 
 

time: 335 us -> 993 us (2.96)
  waiting for transfers between devices: 126 us -> 883 us
  blocking collectives: 102 us -> 0 us
    all_gather x0 -> x1, waiting for transfers between devices: none -> 757 us  [body(): all_gather(partial_grad, ('shot', 'slab'))]
    psum x1 -> x0, blocking collectives: 102 us -> none  [body(): lax.psum(partial_grad, ('shot', 'slab')) * (1.0 / math.sqrt(latent_cells))]
  transfers between devices with their start and end apart: 7 -> 8, of which waited for: 4 -> 5; matrix products, arithmetic and copies ran while one was open for 1% -> 1% of each run, Pallas kernels for 0% -> 0%
where the time goes in v1:
time: 993 us
  waiting for transfers between devices  883 us (89%)
  other arithmetic  62.2 us (6%)
  starting transfers between devices  21.6 us (2%)
  between operations  14.4 us (1%)
    all_gather x1, waiting for transfers between devices, body(): all_gather(partial_grad, ('shot', 'slab'))  757 us
    reduce_scatter x1, waiting for transfers between devices, body(): lax.psum_scatter(image_rows, 'shot', scatter_dimension=0, tiled=True)  118 us
    scatter-add x3, other arithmetic, inject(): field.at[local_x, receivers[0, 1], receivers[0, 2]].add(values, mode='drop')  46.7 us
  transfers between devices with their start and end apart: 8, of which 5 were waited for; matrix products, arithmetic and copies ran while one was open for 1% of the time, Pallas kernels for 0%

profile of v1, /device:TPU:1, one launch (start us, length us, event | category | flops | bytes accessed | tf_op | source)
XLA Modules:
  0.0 992.7 jit_solution(2116766139591605811)
XLA Ops:
  7.2 0.0 copy-start
  7.2 0.0 copy-start.4
  7.2 0.0 copy-start.3
  7.2 0.0 reduce-scatter.2.cloned.1.call-start
  7.2 1.1 slice_bitcast_fusion.1
  8.3 8.8 collective-permute-start
  17.1 1.9 collective-permute-start.1
  19.0 0.7 fusion.67
  19.8 0.7 or_select_fusion
  20.5 0.0 collective-permute-done
  20.5 0.5 collective-permute-done.1
  21.0 0.0 copy-start.6
  21.0 0.7 copy-done.6
  21.6 1.6 select_maximum_fusion.4
  23.2 0.0 copy-done.4
  23.2 0.0 copy-done.3
  23.2 3.7 fusion.13
  26.9 15.6 %scatter_fusion = f32[16,64,128]{2,1,0:T(8,128)S(1)} fusion(f32[16,64,128]{2,1,0:T(8,128)S(1)} %fusion.13, s32[256]{0:T(256)S(1)} %bitcast.58, f32[256]{0:T(256)S(1)} %bitcast.71), kind=kCustom, calls=%fused_computation | custom fusion | flops 256 | bytes 6144 | tf_op jit(solution)/shard_map/scatter-add | solution.py:55
  42.5 4.3 collective-permute-start.3
  46.9 1.9 collective-permute-start.2
  48.8 0.0 collective-permute-done.3
  48.8 0.1 constant_dynamic-update-slice_fusion.1
  48.9 4.2 collective-permute-done.2
  53.1 0.5 select_maximum_fusion.2
  53.7 2.1 fusion.46
  55.8 0.0 copy-start.8
  55.8 15.6 %scatter_fusion.1 = f32[16,64,128]{2,1,0:T(8,128)S(1)} fusion(f32[16,64,128]{2,1,0:T(8,128)S(1)} %fusion.46, s32[256]{0:T(256)S(1)} %bitcast.59, f32[256]{0:T(256)S(1)} %bitcast.70), kind=kCustom, calls=%fused_computation.1 | custom fusion | flops 256 | bytes 6144 | tf_op jit(solution)/shard_map/scatter-add | solution.py:55
  71.4 0.0 copy-start.1
  71.4 1.9 collective-permute-start.5
  73.3 0.0 copy-done.8
  73.3 0.6 fusion.68
  73.9 1.3 compare_and_fusion
  75.2 2.4 collective-permute-start.4
  77.7 0.0 collective-permute-done.5
  77.7 0.1 constant_dynamic-update-slice_fusion.5
  77.8 3.7 collective-permute-done.4
  81.5 0.5 select_maximum_fusion
  82.1 2.1 fusion.36
  84.2 0.0 copy-start.5
  84.2 15.6 %scatter_fusion.2 = f32[16,64,128]{2,1,0:T(8,128)S(1)} fusion(f32[16,64,128]{2,1,0:T(8,128)S(1)} %fusion.36, s32[256]{0:T(256)S(1)} %bitcast.60, f32[256]{0:T(256)S(1)} %bitcast.69), kind=kCustom, calls=%fused_computation.2 | custom fusion | flops 256 | bytes 6144 | tf_op jit(solution)/shard_map/scatter-add | solution.py:55
  99.8 0.0 copy-done.1
  99.8 0.0 copy-done.5
  99.8 0.0 copy-start.2
  99.8 0.0 copy-start.7
  99.8 0.3 fusion.58
  100.1 1.1 copy.23
  101.2 0.0 copy-done.2
  101.2 0.0 reduce-scatter.2.cloned.1.call-update
  101.2 0.2 all-gather.4.cloned.1.call-start
  101.5 0.0 copy-done.7
  101.5 0.2 reshape.127
  101.7 117.9 %reduce-scatter.2.cloned.1.call-done = f32[4,16,128]{2,1,0:T(8,128)} async-done(((f32[64,16,128]{2,1,0:T(8,128)}), f32[4,16,128]{2,1,0:T(8,128)}) %reduce-scatter.2.cloned.1.call-update) | async-done | bytes 32784 | tf_op jit(solution)/shard_map/reduce_scatter | solution.py:76
  219.6 2.8 reshape.124
  222.4 0.7 copy.24
  223.1 0.9 convolution_bitcast_fusion.1
  224.0 0.0 all-gather.4.cloned.1.call-update
  224.1 0.0 copy-done
  224.1 1.0 convolution_bitcast_fusion
  225.1 0.2 copy.31
  225.3 1.0 reshape.155
  226.3 756.9 %all-gather.4.cloned.1.call-done = f32[512,64,8]{1,2,0:T(8,128)} async-done(((f32[1,64,8]{1,2,0:T(8,128)}), f32[512,64,8]{1,2,0:T(8,128)}) %all-gather.4.cloned.1.call-update) | async-done | bytes 1048592 | tf_op jit(solution)/shard_map/all_gather | solution.py:94
  983.2 2.1 reduce_sum.9
  985.3 0.6 broadcast_multiply_fusion
  (6 shorter events, 0.1 us)
Async XLA Ops:
  7.2 216.9 %copy-start = (f32[64,8]{0,1:T(8,128)S(1)}, f32[64,8]{0,1:T(8,128)}, u32[]{:S(2)}) copy-start(f32[64,8]{0,1:T(8,128)} %param.17) | copy-start | bytes 6148
  7.2 16.0 %copy-start.4 = (f32[1,16,64,128]{3,2,1,0:T(8,128)S(1)}, f32[1,16,64,128]{3,2,1,0:T(8,128)}, u32[]{:S(2)}) copy-start(f32[1,16,64,128]{3,2,1,0:T(8,128)} %param.9) | copy-start | bytes 1572868
  7.2 16.0 %copy-start.3 = (f32[16,64,128]{2,1,0:T(8,128)S(1)}, f32[16,64,128]{2,1,0:T(8,128)}, u32[]{:S(2)}) copy-start(f32[16,64,128]{2,1,0:T(8,128)} %param.11) | copy-start | bytes 1572868
  7.2 212.4 %reduce-scatter.2.cloned.1.call-start = ((), (), s32[]{:S(2)}) async-start(), calls=%async_computation.1 | async-start | bytes 557056 | tf_op jit(solution)/shard_map/reduce_scatter | solution.py:76
  8.3 12.2 %collective-permute-start = (f32[4,64,128]{2,1,0:T(8,128)S(1)}, f32[4,64,128]{2,1,0:T(8,128)S(1)}, u32[]{:S(2)}, u32[]{:S(2)}) collective-permute-start(f32[4,64,128]{2,1,0:T(8,128)S(1)} %get-tuple-element.24), channel_id=1, source_target_pairs={{1,0},{2,1},{3,2},{4,3},{5,4},{6,5},{7,6},{8,7},{9,8},{10,9},{11,1... | collective-permute-start | bytes 393224 | tf_op jit(solution)/shard_map/ppermute | solution.py:20
  17.1 3.9 collective-permute-start.1
  21.0 0.7 copy-start.6
  42.5 6.3 collective-permute-start.3
  46.9 6.3 collective-permute-start.2
  55.8 17.5 %copy-start.8 = (s32[1,2]{1,0:T(1,128)S(1)}, s32[1,2]{1,0:T(1,128)}, u32[]{:S(2)}) copy-start(s32[1,2]{1,0:T(1,128)} %param.15) | copy-start | bytes 28
  71.4 28.4 %copy-start.1 = (f32[16,64,128]{2,1,0:T(8,128)}, f32[16,64,128]{2,1,0:T(8,128)S(1)}, u32[]{:S(2)}) copy-start(f32[16,64,128]{2,1,0:T(8,128)S(1)} %scatter_fusion.1) | copy-start | bytes 1572868
  71.4 6.2 collective-permute-start.5
  75.2 6.3 collective-permute-start.4
  84.2 15.6 %copy-start.5 = (bf16[1,3,16,64,128]{4,3,2,1,0:T(8,128)(2,1)S(1)}, bf16[1,3,16,64,128]{4,3,2,1,0:T(8,128)(2,1)}, u32[]{:S(2)}) copy-start(bf16[1,3,16,64,128]{4,3,2,1,0:T(8,128)(2,1)} %param.12) | copy-start | bytes 2359300
  99.8 1.4 copy-start.2
  99.8 1.7 copy-start.7
  101.2 881.9 %all-gather.4.cloned.1.call-start = ((), (), s32[]{:S(2)}) async-start(), calls=%async_computation.2 | async-start | bytes 2101248 | tf_op jit(solution)/shard_map/all_gather | solution.py:94
Sparse Core Ops, SparseCore 0:
  101.3 118.1 reduce-scatter.1
  224.2 758.9 all-gather.3
